TPU v7x, 32 devices: a whole 2x2x4 slice. The times are simulated.
32 devices in a mesh: rep: 8 (over z, x), atom: 4 (over y, core).
Axes of the slice: x: 2, y: 2, z: 4, core: 2. Of those that a mesh axis runs over, the one named last changes fastest.
Arguments:
- starting_locations: float32 [32, 3, 4096], P('rep', None, 'atom'), may hold values from 0 to 4
- starting_speeds: float32 [32, 3, 4096], P('rep', None, 'atom'), may hold values from -5 to 5
- terminal_location_adjoint: float32 [32, 3, 4096], P('rep', None, 'atom'), may hold values from -6 to 6
- terminal_speed_adjoint: float32 [32, 3, 4096], P('rep', None, 'atom'), may hold values from -7.5 to 7.5
- interaction_strength: float32 [4096], P('atom'), may hold values from 0.5 to 2
- reciprocal_particle_weight: float32 [4096], P('atom'), may hold values from 0.05 to 2
- heat_levels: float32 [32], P('rep'), may hold values from 0.25 to 4
- swap_indicator: int32 [32], P('rep'), may hold values from 0 to 1, as said below
- companion_group_indices: int32 [5, 32, 2], P(None, 'atom'), may hold values from 0 to 23, as said below
Outputs:
- final_pos: float32 [32, 3, 4096], P('rep', None, 'atom')
- final_vel: float32 [32, 3, 4096], P('rep', None, 'atom')
- energies: float32 [32], P('rep')
- grad_pos: float32 [32, 3, 4096], P('rep', None, 'atom')
- grad_vel: float32 [32, 3, 4096], P('rep', None, 'atom')
- grad_coupling: float32 [4096], P('atom')
Inputs may be any that keep to these rules, and one draw needn't show every extreme that they name: `swap_indicator`: replicas r and r + 4, for r with r // 4 even, carry the same flag; among the replicas r to r + 3, for r a multiple of 8, at least one carries 1. `companion_group_indices`: the 2 entries of a row differ.
All inputs are finite; a program needn't handle non-finite values.
Results may differ from a plain program's by a relative error of at most 0.0003.
Values sent between devices are 32-bit elements; how exact they have to be, the bound alone decides.
A program may use at most 64 MiB of HBM per device.

v0:
```python
import functools
import math

import jax
import jax.numpy as jnp
from jax import lax
from jax.experimental import pallas as pl
from jax.experimental.pallas import tpu as pltpu
from jax.sharding import PartitionSpec as P

TIME_STEP = 0.05
THERMO_RELAX = 0.5
KINETIC_EPSILON = 1e-06


def with_halo(block, sides, width):
    for axis, dim in sides:
        count = lax.axis_size(axis)
        forward = [(i, i + 1) for i in range(count - 1)]
        backward = [(target, source) for source, target in forward]
        low = lax.ppermute(
            lax.slice_in_dim(block, block.shape[dim] - width, None, axis=dim), axis, forward
        )
        high = lax.ppermute(lax.slice_in_dim(block, 0, width, axis=dim), axis, backward)
        block = jnp.concatenate([low, block, high], axis=dim)
    return block


def from_partner(x, axis, apart):
    return lax.ppermute(x, axis, [(i, i ^ 1 << apart) for i in range(lax.axis_size(axis))])


def split_blocks(extended, block_count):
    block_width = extended.shape[2] // (3 * block_count)
    return extended.reshape(extended.shape[0], 4, 3 * block_count, block_width)


def pair_terms(blocks, own_start, far_ids, keep):
    block_count = far_ids.shape[0]
    partners = far_ids.shape[1]
    block_width = blocks.shape[3]
    own_block = blocks[:, :, own_start : own_start + block_count]
    far_block = jnp.take(blocks, far_ids, axis=2)
    squared = jnp.zeros(
        (blocks.shape[0], block_count, partners, block_width, block_width), jnp.float32
    )
    for axis_id in range(3):
        offset = own_block[:, axis_id, :, None, :, None] - far_block[:, axis_id, :, :, None, :]
        squared = squared + offset * offset
    own_ids = own_start + jnp.arange(block_count, dtype=jnp.int32)
    self_block = far_ids == own_ids[:, None]
    diagonal = jnp.arange(block_width)[:, None] == jnp.arange(block_width)[None, :]
    kept_pairs = keep[:, :, None, None] * (
        1.0 - (self_block[:, :, None, None] & diagonal).astype(jnp.float32)
    )
    weight = own_block[:, 3, :, None, :, None] * far_block[:, 3, :, :, None, :]
    strength = block_count / (8.0 * partners)
    return (
        0.5 * strength * jnp.sum(weight * jnp.exp(-0.5 * squared) * kept_pairs, axis=(1, 2, 3, 4))
    )


def energy_of(extended, companion_group_indices, beside_all, iteration_number):
    lists_now = companion_group_indices[iteration_number]
    block_count = lists_now.shape[0]
    blocks = split_blocks(extended, block_count)
    per_walker = pair_terms(blocks, block_count, lists_now, jnp.ones(lists_now.shape, jnp.float32))
    total = jnp.sum(per_walker)
    return (total, per_walker)


def widen(layer):
    return with_halo(layer, (("atom", 2),), layer.shape[2])


def settle(gradient):
    block_width = gradient.shape[2] // 3
    padded = with_halo(gradient, (("atom", 2),), block_width)
    return (
        padded[:, :, 2 * block_width : 3 * block_width]
        + padded[:, :, :block_width]
        + padded[:, :, 4 * block_width :]
    )


def atom_total(partial_value):
    return lax.psum(partial_value, "atom")


def force_from(particle_location, interaction_strength, companion_group_indices, iteration_number):
    column = jnp.broadcast_to(
        interaction_strength[None, None, :],
        (particle_location.shape[0], 1, particle_location.shape[2]),
    )
    extended = widen(jnp.concatenate([particle_location, column], axis=1))
    (collapsed_total, per_walker), gradient = jax.value_and_grad(energy_of, has_aux=True)(
        extended, companion_group_indices, None, iteration_number
    )
    return (-settle(gradient[:, :3]), per_walker, extended)


def force_back(cot_force, extended, companion_group_indices, iteration_number):

    def slope_of(widened):
        return jax.grad(energy_of, has_aux=True)(
            widened, companion_group_indices, None, iteration_number
        )[0][:, :3]

    slope_now, pullback = jax.vjp(slope_of, extended)
    cot_extended = pullback(-widen(cot_force))[0]
    returned = settle(cot_extended)
    return (returned[:, :3], jnp.sum(returned[:, 3], axis=0))


def local_general(
    starting_locations,
    starting_speeds,
    terminal_location_adjoint,
    terminal_speed_adjoint,
    interaction_strength,
    reciprocal_particle_weight,
    heat_levels,
    swap_indicator,
    companion_group_indices,
):
    half_step = 0.5 * TIME_STEP
    atoms_all = starting_locations.shape[2] * lax.axis_size("atom")
    mass_row = reciprocal_particle_weight[None, None, :]
    steps_all = companion_group_indices.shape[0] - 1
    swap_at = steps_all // 2
    push_vectors, energy, extended = force_from(
        starting_locations, interaction_strength, companion_group_indices, 0
    )
    saved_extended = [extended]
    saved_updated = []
    saved_factor = []
    saved_current = []
    stored_goal = []
    particle_location, particle_speed = (starting_locations, starting_speeds)
    desired_heat_level = heat_levels
    partner_temp = from_partner(heat_levels, "rep", 0)
    upcoming_heat_level = jnp.where(swap_indicator == 1, partner_temp, heat_levels)
    interaction_multiplier = jnp.sqrt(upcoming_heat_level / heat_levels)[:, None, None]
    for iteration_number in range(steps_all):
        if iteration_number == swap_at:
            particle_speed = particle_speed * interaction_multiplier
            desired_heat_level = upcoming_heat_level
        mid_velocity = particle_speed + half_step * mass_row * push_vectors
        particle_location = particle_location + TIME_STEP * mid_velocity
        push_vectors, energy, extended = force_from(
            particle_location, interaction_strength, companion_group_indices, iteration_number + 1
        )
        updated = mid_velocity + half_step * mass_row * push_vectors
        kinetic, energy = atom_total(
            (0.5 * jnp.sum(updated * updated / mass_row, axis=(1, 2)), energy)
        )
        present_state = 2.0 * kinetic / (3 * atoms_all) + KINETIC_EPSILON
        rescaling_multiplier = jnp.sqrt(
            1.0 + THERMO_RELAX * (desired_heat_level / present_state - 1.0)
        )
        particle_speed = rescaling_multiplier[:, None, None] * updated
        saved_extended.append(extended)
        saved_updated.append(updated)
        saved_factor.append(rescaling_multiplier)
        saved_current.append(present_state)
        stored_goal.append(desired_heat_level)
    energies = energy / atoms_all
    cot_x, cot_v = (terminal_location_adjoint, terminal_speed_adjoint)
    cot_f = jnp.zeros_like(cot_x)
    cot_coupling = jnp.zeros_like(interaction_strength)
    for iteration_number in reversed(range(steps_all)):
        updated = saved_updated[iteration_number]
        rescaling_multiplier = saved_factor[iteration_number]
        present_state = saved_current[iteration_number]
        desired_heat_level = stored_goal[iteration_number]
        inner_sum = atom_total(jnp.sum(cot_v * updated, axis=(1, 2)))
        slope_factor = (
            -THERMO_RELAX
            * desired_heat_level
            / (present_state * present_state)
            * (2.0 / (3 * atoms_all))
            / (2.0 * rescaling_multiplier)
        )
        cot_updated = (
            rescaling_multiplier[:, None, None] * cot_v
            + (inner_sum * slope_factor)[:, None, None] * updated / mass_row
        )
        cot_force_now = cot_f + half_step * mass_row * cot_updated
        returned_x, returned_c = force_back(
            cot_force_now,
            saved_extended[iteration_number + 1],
            companion_group_indices,
            iteration_number + 1,
        )
        cot_coupling = cot_coupling + returned_c
        cot_x = cot_x + returned_x
        cot_mid = cot_updated + TIME_STEP * cot_x
        cot_v = cot_mid
        cot_f = half_step * mass_row * cot_mid
        if iteration_number == swap_at:
            cot_v = cot_v * interaction_multiplier
    returned_x, returned_c = force_back(cot_f, saved_extended[0], companion_group_indices, 0)
    cot_x = cot_x + returned_x
    cot_coupling = cot_coupling + returned_c
    grad_coupling = lax.psum(cot_coupling, "rep")
    return (particle_location, particle_speed, energies, cot_x, cot_v, grad_coupling)


LOG2E = math.log2(math.e)
ROWS = 16
KDIST = 32
KCROSS = 48
UNROLL = 4


def split3(x):
    hi = x.astype(jnp.bfloat16).astype(jnp.float32)
    rest = x - hi
    mid = rest.astype(jnp.bfloat16).astype(jnp.float32)
    low = (rest - mid).astype(jnp.bfloat16).astype(jnp.float32)
    return hi, mid, low


def row_sum(x):
    return jnp.sum(x, axis=1, keepdims=True)


def whole_sum(x):
    return jnp.full((1, x.shape[-1]), jnp.sum(x), jnp.float32)


def replica_kernel(
    far_ref,
    temp_ref,
    x0_ref,
    v0_ref,
    cx_ref,
    cv_ref,
    c_ref,
    m_ref,
    xf_ref,
    vf_ref,
    en_ref,
    gx_ref,
    gv_ref,
    gc_ref,
    left,
    right,
    left_w,
    right_w,
    rows_w,
    rows_x,
    rows_g,
    weights,
    acc_w,
    acc_v,
    out_w,
    out_v,
    saved_u,
    f_ref,
    fac_ref,
    cur_ref,
):
    nb, _, width = x0_ref.shape
    evals = rows_x.shape[0]
    steps = evals - 1
    partners = 2
    half = 0.5 * TIME_STEP
    block_count = temp_ref[2]
    dof = float(3 * nb * width)
    f32, bf16 = jnp.float32, jnp.bfloat16
    real = slice(0, nb)
    t_first = jnp.full((1, width), temp_ref[0], f32)
    t_last = jnp.full((1, width), temp_ref[1], f32)
    swap_gain = jnp.sqrt(t_last / t_first)
    strength = 0.5 * block_count / (8.0 * partners)
    log_scale = jnp.log(strength * jnp.ones((1, width), f32)) * LOG2E
    mass = m_ref[...]

    for ref in (left_w, right_w, rows_w):
        ref[...] = jnp.zeros_like(ref)
    rows_x[...] = jnp.zeros_like(rows_x)
    rows_g[...] = jnp.zeros_like(rows_g)

    def put(ref, at, value):
        ref[real, at : at + value.shape[1], :] = value

    one = jnp.ones((nb, 1, width), f32)
    zero_pad = (((0,), (0,)), ((), ()))

    def pair(ref, n, p):
        base = (n * nb + p) * partners
        return jnp.concatenate([ref[far_ref[base]], ref[far_ref[base + 1]]], axis=1)

    def scatter(out, acc, n):
        for p in range(nb):
            base = (n * nb + p) * partners
            for k in range(partners):
                q = far_ref[base + k]
                acc[q] = acc[q] + out[p, :, k * width : (k + 1) * width]

    def set_rows(dest, value):
        hi, mid, low = split3(value)
        put(rows_w, 0, hi)
        put(rows_w, 3, mid)
        put(rows_w, 6, low)
        put(rows_w, 9, one)
        dest[...] = rows_w[...].astype(bf16)

    def products(first, second, at):
        for i, j in ((0, 0), (0, 1), (1, 0), (0, 2), (1, 1), (2, 0)):
            put(left_w, at, first[i])
            put(right_w, at, second[j])
            at += first[0].shape[1]
        return at

    def singles(ref, other, value, at):
        for part in split3(value):
            put(ref, at, part)
            put(other, at, one)
            at += 1
        return at

    def force(x, n):
        set_rows(rows_x.at[n], x)
        self_term = -0.5 * LOG2E * row_sum(x * x) + jnp.log(c_ref[...]) * LOG2E
        at = products(split3(x * LOG2E), split3(x), 0)
        at = singles(left_w, right_w, self_term + log_scale, at)
        at = singles(right_w, left_w, self_term, at)
        right_w[nb, at - 3 : at - 2, :] = jnp.full((1, width), -1e6, f32)
        left[:, 0:KDIST, :] = left_w[real, 0:KDIST, :].astype(bf16)
        right[:, 0:KDIST, :] = right_w[:, 0:KDIST, :].astype(bf16)

        @pl.loop(0, nb // UNROLL)
        def _(chunk):
            for i in range(UNROLL):
                p = chunk * UNROLL + i
                exponent = lax.dot_general(
                    left[p, 0:KDIST, :],
                    pair(right.at[:, 0:KDIST, :], n, p),
                    zero_pad,
                    preferred_element_type=f32,
                )
                w = jnp.exp2(exponent).astype(bf16)
                weights[n, p] = w
                out_w[p] = jnp.dot(rows_x[n, p], w, preferred_element_type=f32)
                acc_w[p] = lax.dot_general(
                    pair(rows_x.at[n], n, p),
                    w,
                    (((1,), (1,)), ((), ())),
                    preferred_element_type=f32,
                )

        scatter(out_w, acc_w, n)
        pulled = acc_w[real, 0:3, :] + acc_w[real, 3:6, :] + acc_w[real, 6:9, :]
        f_ref[...] = x * acc_w[real, 9:10, :] - pulled

    def force_back(g, n):
        x = (
            rows_x[n, real].astype(f32)[:, 0:3]
            + rows_x[n, real].astype(f32)[:, 3:6]
            + rows_x[n, real].astype(f32)[:, 6:9]
        )
        set_rows(rows_g, g)
        sx, sg = split3(x), split3(g)
        neg_g = tuple(-part for part in sg)
        neg_x = tuple(-part for part in sx)
        at = products(sx, neg_g, 0)
        at = products(sg, neg_x, at)
        own = row_sum(x * g)
        at = singles(left_w, right_w, own, at)
        singles(right_w, left_w, own, at)
        left[...] = left_w[real].astype(bf16)
        right[...] = right_w[...].astype(bf16)

        @pl.loop(0, nb // UNROLL)
        def _(chunk):
            for i in range(UNROLL):
                p = chunk * UNROLL + i
                phi = lax.dot_general(
                    left[p], pair(right, n, p), zero_pad, preferred_element_type=f32
                )
                w = weights[n, p]
                v = (w.astype(f32) * phi).astype(bf16)
                out_w[p] = jnp.dot(rows_g[p], w, preferred_element_type=f32)
                out_v[p] = jnp.dot(rows_x[n, p], v, preferred_element_type=f32)
                acc_w[p] = lax.dot_general(
                    pair(rows_g, n, p),
                    w,
                    (((1,), (1,)), ((), ())),
                    preferred_element_type=f32,
                )
                acc_v[p] = lax.dot_general(
                    pair(rows_x.at[n], n, p),
                    v,
                    (((1,), (1,)), ((), ())),
                    preferred_element_type=f32,
                )

        scatter(out_w, acc_w, n)
        scatter(out_v, acc_v, n)
        pulled_w = acc_w[real, 0:3, :] + acc_w[real, 3:6, :] + acc_w[real, 6:9, :]
        pulled_v = acc_v[real, 0:3, :] + acc_v[real, 3:6, :] + acc_v[real, 6:9, :]
        total_v = acc_v[real, 9:10, :]
        back_x = g * acc_w[real, 9:10, :] - pulled_w - x * total_v + pulled_v
        return back_x, total_v

    x, v, goal = x0_ref[...], v0_ref[...], t_first
    force(x, 0)
    for n in range(steps):
        if n == steps // 2:
            v = v * swap_gain
            goal = t_last
        mid = v + half * mass * f_ref[...]
        x = x + TIME_STEP * mid
        force(x, n + 1)
        u = mid + half * mass * f_ref[...]
        kinetic = 0.5 * whole_sum(u * u / mass)
        current = 2.0 * kinetic / dof + KINETIC_EPSILON
        factor = jnp.sqrt(1.0 + THERMO_RELAX * (goal / current - 1.0))
        v = factor * u
        saved_u[n] = u
        fac_ref[n] = factor
        cur_ref[n] = current
    xf_ref[...] = x
    vf_ref[...] = v
    coupling = c_ref[...]
    selfs = jnp.zeros((1, width), f32)
    square = strength * jnp.sum(coupling * coupling, axis=1)
    owned = jnp.zeros((1, width), f32)
    for p in range(nb):
        base = (steps * nb + p) * partners
        for k in range(partners):
            hit = (far_ref[base + k] == p).astype(f32)
            selfs = selfs + hit * square[p : p + 1]
    total = whole_sum(acc_w[real, 9:10, :]) * 0.5 - whole_sum(selfs)
    en_ref[...] = total / float(nb * width)

    cot_x, cot_v = cx_ref[...], cv_ref[...]
    cot_f = jnp.zeros_like(cot_x)
    cot_c = jnp.zeros((nb, 1, width), f32)
    for n in reversed(range(steps)):
        goal = t_last if n >= steps // 2 else t_first
        u, factor, current = saved_u[n], fac_ref[n], cur_ref[n]
        inner = whole_sum(cot_v * u)
        slope = -THERMO_RELAX * goal / (current * current) * (2.0 / dof) / (2.0 * factor)
        cot_u = factor * cot_v + (inner * slope) * u / mass
        back_x, back_c = force_back(cot_f + half * mass * cot_u, n + 1)
        cot_c = cot_c + back_c
        cot_x = cot_x + back_x
        cot_mid = cot_u + TIME_STEP * cot_x
        cot_v = cot_mid
        cot_f = half * mass * cot_mid
        if n == steps // 2:
            cot_v = cot_v * swap_gain
    back_x, back_c = force_back(cot_f, 0)
    gx_ref[...] = cot_x + back_x
    gv_ref[...] = cot_v
    gc_ref[...] = (cot_c + back_c) / coupling


def run_replica(far, temps, x0, v0, cx, cv, coupling, mass, evals):
    nb, _, width = x0.shape
    f32, bf16 = jnp.float32, jnp.bfloat16
    vec = jax.ShapeDtypeStruct((nb, 3, width), f32)
    vmem = pl.BlockSpec(memory_space=pltpu.VMEM)
    smem = pl.BlockSpec(memory_space=pltpu.SMEM)
    return pl.pallas_call(
        replica_kernel,
        out_shape=(
            vec,
            vec,
            jax.ShapeDtypeStruct((1, width), f32),
            vec,
            vec,
            jax.ShapeDtypeStruct((nb, 1, width), f32),
        ),
        in_specs=[smem, smem] + [vmem] * 6,
        out_specs=[vmem] * 6,
        scratch_shapes=[
            pltpu.VMEM((nb, KCROSS, width), bf16),
            pltpu.VMEM((nb + 1, KCROSS, width), bf16),
            pltpu.VMEM((nb + 1, KCROSS, width), f32),
            pltpu.VMEM((nb + 1, KCROSS, width), f32),
            pltpu.VMEM((nb + 1, ROWS, width), f32),
            pltpu.VMEM((evals, nb + 1, ROWS, width), bf16),
            pltpu.VMEM((nb + 1, ROWS, width), bf16),
            pltpu.VMEM((evals, nb, width, 2 * width), bf16),
            pltpu.VMEM((nb + 1, ROWS, width), f32),
            pltpu.VMEM((nb + 1, ROWS, width), f32),
            pltpu.VMEM((nb, ROWS, 2 * width), f32),
            pltpu.VMEM((nb, ROWS, 2 * width), f32),
            pltpu.VMEM((evals - 1, nb, 3, width), f32),
            pltpu.VMEM((nb, 3, width), f32),
            pltpu.VMEM((evals - 1, 1, width), f32),
            pltpu.VMEM((evals - 1, 1, width), f32),
        ],
        compiler_params=pltpu.CompilerParams(vmem_limit_bytes=60 * 1024 * 1024),
    )(far, temps, x0, v0, cx, cv, coupling, mass)


def local_whole(
    starting_locations,
    starting_speeds,
    terminal_location_adjoint,
    terminal_speed_adjoint,
    interaction_strength,
    reciprocal_particle_weight,
    heat_levels,
    swap_indicator,
    companion_group_indices,
):
    evals, blocks, partners = companion_group_indices.shape
    owners = lax.axis_size("atom")
    me = lax.axis_index("atom")
    atoms = starting_locations.shape[2]
    width = atoms // blocks
    nb = owners * blocks
    packed = jnp.concatenate(
        [
            starting_locations,
            starting_speeds,
            terminal_location_adjoint,
            terminal_speed_adjoint,
        ],
        axis=1,
    )
    mine = lax.all_to_all(packed, "atom", 0, 0, tiled=True)
    mine = mine.reshape(owners, 12, blocks, width).transpose(0, 2, 1, 3).reshape(nb, 12, width)
    shared = lax.all_gather(
        jnp.stack([interaction_strength, reciprocal_particle_weight]), "atom", axis=0
    )
    coupling = shared[:, 0].reshape(nb, 1, width)
    mass = shared[:, 1].reshape(nb, 1, width)
    slots = lax.all_gather(companion_group_indices, "atom", axis=1, tiled=True)
    block_ids = jnp.arange(nb, dtype=jnp.int32)
    far = (block_ids // blocks * blocks - blocks)[None, :, None] + slots
    far = jnp.where((far >= 0) & (far < nb), far, nb).reshape(-1)
    partner_temp = from_partner(heat_levels, "rep", 0)
    upcoming = jnp.where(swap_indicator == 1, partner_temp, heat_levels)
    temps = jnp.stack(
        [
            lax.dynamic_index_in_dim(heat_levels, me, keepdims=False),
            lax.dynamic_index_in_dim(upcoming, me, keepdims=False),
            jnp.float32(blocks),
        ]
    )
    xf, vf, en, gx, gv, gc = run_replica(
        far,
        temps,
        mine[:, 0:3],
        mine[:, 3:6],
        mine[:, 6:9],
        mine[:, 9:12],
        coupling,
        mass,
        evals,
    )
    done = jnp.concatenate([xf, vf, gx, gv], axis=1)
    done = done.reshape(owners, blocks, 12, width).transpose(0, 2, 1, 3).reshape(owners, 12, atoms)
    done = lax.all_to_all(done, "atom", 0, 0, tiled=True)
    energies = lax.all_gather(en[0, 0:1], "atom", axis=0, tiled=True)
    part = lax.psum_scatter(gc.reshape(-1), "atom", scatter_dimension=0, tiled=True)
    grad_coupling = lax.psum(part, "rep")
    return (done[:, 0:3], done[:, 3:6], energies, done[:, 6:9], done[:, 9:12], grad_coupling)


def local(*args):
    partners = args[8].shape[2]
    if args[0].shape[0] == lax.axis_size("atom") and partners == 2:
        return local_whole(*args)
    return local_general(*args)


def solution(mesh):
    in_specs = (
        P("rep", None, "atom"),
        P("rep", None, "atom"),
        P("rep", None, "atom"),
        P("rep", None, "atom"),
        P("atom"),
        P("atom"),
        P("rep"),
        P("rep"),
        P(None, "atom", None),
    )
    out_specs = (
        P("rep", None, "atom"),
        P("rep", None, "atom"),
        P("rep"),
        P("rep", None, "atom"),
        P("rep", None, "atom"),
        P("atom"),
    )
    return jax.shard_map(local, mesh=mesh, in_specs=in_specs, out_specs=out_specs, check_vma=False)
```

profile of v0, /device:TPU:0, one launch (start us, length us, event | category | flops | bytes accessed | tf_op | source)
XLA Modules:
  0.0 136.4 jit_solution(18208946642034573337)
XLA Ops:
  0.6 3.0 %collective-permute-start = (f32[4]{0:T(128)}, f32[4]{0:T(128)S(1)}, u32[]{:S(2)}, u32[]{:S(2)}) collective-permute-start(f32[4]{0:T(128)} %param.15), channel_id=1, source_target_pairs={{0,4},{4,0},{8,12},{12,8},{16,20},{20,16},{24,28},{28,24},{1,5},{5... | collective-permute-start | bytes 56 | tf_op jit(solution)/shard_map/ppermute | solution.py:30
  3.7 0.8 copy.22
  4.6 0.7 copy-done.1
  5.4 0.8 copy-done.2
  6.2 0.8 pad_maximum_fusion
  6.9 3.5 %all-to-all-start = ((f32[4,12,1024]{2,1,0:T(8,128)}), f32[4,12,1024]{2,1,0:T(8,128)S(1)}, u32[]{:S(2)}, u32[]{:S(2)}) async-start(f32[4,12,1024]{2,1,0:T(8,128)} %pad_maximum_fusion), calls=%async_computation | async-start | bytes 524288 | tf_op jit(solution)/shard_map/all_to_all | solution.py:528
  11.2 6.3 %all-gather.2 = f32[4,2,1024]{2,1,0:T(2,128)S(1)} all-gather(f32[1,2,1024]{2,1,0:T(2,128)S(1)} %maximum_bitcast_fusion), channel_id=2, replica_groups=mesh['rep'=8,'atom'=4] {'atom'}, dimensions={0}, use_global_device_ids=true | all-gather | bytes 40960 | tf_op jit(solution)/shard_map/all_gather | solution.py:530
  17.5 0.6 fusion.4
  18.3 5.2 %all_gather.12 = s32[5,32,2]{0,2,1:T(2,128)S(1)} all-gather(s32[5,8,2]{0,2,1:T(2,128)S(1)} %copy.20), channel_id=1, replica_groups=mesh['rep'=8,'atom'=4] {'atom'}, dimensions={1}, use_global_device_ids=true | all-gather | bytes 1600 | tf_op jit(solution)/shard_map/all_gather | solution.py:535
  23.9 0.7 reshape.45.far_ref
  25.2 1.9 %pad_maximum_fusion.2.temp_ref = f32[3]{0:T(128)} fusion(f32[1]{0:T(128)} %constant.39.clone.1, f32[1]{0:T(128)} %dynamic_slice.8, f32[1]{0:T(128)} %dynamic_slice.7), kind=kLoop, calls=%fused_computation.11 | loop fusion | flops 6 | bytes 24 | tf_op jit(solution)/shard_map/stack | solution.py:541
  27.2 0.7 fusion.3
  27.9 64.3 %shard_map.136 = (f32[32,3,128]{2,1,0:T(4,128)}, f32[32,3,128]{2,1,0:T(4,128)}, f32[1,128]{1,0:T(1,128)}, f32[32,3,128]{2,1,0:T(4,128)}, f32[32,3,128]{2,1,0:T(4,128)}, /*index=5*/f32[32,1,128]{2,1,0:T(1,128)}) custom-call(s32[320]{0:T(512)} %reshape.45.far_ref, f32[3]{0:T(128)} %pad_maximum_fusion.2.temp_ref, f32[32,3,128]{2,1,0:T(4,128)} %get-tuple-element.33.x0_ref, ...), custom_call_target="tpu_custom_call" | custom-call | tf_op jit(solution)/shard_map/pallas_call | solution.py:468
  92.2 1.0 pad_maximum_fusion.1
  93.3 0.7 reshape.49
  94.0 3.5 %all-to-all-start.1 = ((f32[4,12,1024]{2,1,0:T(8,128)}), f32[4,12,1024]{2,1,0:T(8,128)S(1)}, u32[]{:S(2)}, u32[]{:S(2)}) async-start(f32[4,12,1024]{2,1,0:T(8,128)} %reshape.49), calls=%async_computation.1 | async-start | bytes 524288 | tf_op jit(solution)/shard_map/all_to_all | solution.py:561
  98.8 0.6 copy-done.10
  99.5 0.7 bitcast_dynamic-update-slice_fusion
  100.2 12.3 %all-reduce.2 = (f32[4]{0:T(128)}, f32[4096]{0:T(1024)S(1)}) all-reduce(f32[4]{0:T(128)S(1)} %bitcast_dynamic-update-slice_fusion, f32[4096]{0:T(1024)S(1)} %bitcast.24), channel_id=3, replica_groups=mesh['rep'=8,'atom'=4] {'atom'}, use_global_device_ids=true, to_apply=%add | all-reduce | flops 4100 | bytes 32800 | tf_op jit(solution)/shard_map/all_gather | solution.py:562
  112.4 21.3 %psum.7 = f32[1024]{0:T(1024)} all-reduce(f32[1024]{0:T(1024)S(1)} %dynamic-slice.2), channel_id=1, replica_groups=mesh['rep'=8,'atom'=4] {'rep'}, use_global_device_ids=true, to_apply=%region_1.2 | all-reduce | flops 1024 | bytes 8192 | tf_op jit(solution)/shard_map/psum | solution.py:564
  133.7 0.7 copy.28
  134.4 0.7 copy.29
  135.1 0.7 copy.30
  135.7 0.7 copy.31
  (40 shorter events, 2.8 us)
Async XLA Ops:
  0.6 3.9 %copy-start = (f32[4,3,1024]{2,0,1:T(4,128)S(1)}, f32[4,3,1024]{2,0,1:T(4,128)}, u32[]{:S(2)}) copy-start(f32[4,3,1024]{2,0,1:T(4,128)} %param.10) | copy-start | bytes 147460
  0.6 24.0 %collective-permute-start = (f32[4]{0:T(128)}, f32[4]{0:T(128)S(1)}, u32[]{:S(2)}, u32[]{:S(2)}) collective-permute-start(f32[4]{0:T(128)} %param.15), channel_id=1, source_target_pairs={{0,4},{4,0},{8,12},{12,8},{16,20},{20,16},{24,28},{28,24},{1,5},{5... | collective-permute-start | bytes 56 | tf_op jit(solution)/shard_map/ppermute | solution.py:30
  4.5 0.8 copy-start.1
  5.3 0.8 copy-start.2
  6.9 3.6 %copy-start.8 = (f32[4]{0:T(128)S(1)}, f32[4]{0:T(128)}, u32[]{:S(2)}) copy-start(f32[4]{0:T(128)} %param.15) | copy-start | bytes 52
  6.9 20.2 %all-to-all-start = ((f32[4,12,1024]{2,1,0:T(8,128)}), f32[4,12,1024]{2,1,0:T(8,128)S(1)}, u32[]{:S(2)}, u32[]{:S(2)}) async-start(f32[4,12,1024]{2,1,0:T(8,128)} %pad_maximum_fusion), calls=%async_computation | async-start | bytes 524288 | tf_op jit(solution)/shard_map/all_to_all | solution.py:528
  10.5 0.7 copy-start.6
  10.5 0.7 copy-start.5
  17.5 0.7 copy-start.4
  23.9 0.7 copy-start.9
  94.0 3.6 %copy-start.7 = (u32[32]{0:T(128)S(1)}, u32[32]{0:T(128)}, u32[]{:S(2)}) copy-start(u32[32]{0:T(128)} %constant.48) | copy-start | bytes 388
  94.0 39.7 %all-to-all-start.1 = ((f32[4,12,1024]{2,1,0:T(8,128)}), f32[4,12,1024]{2,1,0:T(8,128)S(1)}, u32[]{:S(2)}, u32[]{:S(2)}) async-start(f32[4,12,1024]{2,1,0:T(8,128)} %reshape.49), calls=%async_computation.1 | async-start | bytes 524288 | tf_op jit(solution)/shard_map/all_to_all | solution.py:561
  97.6 2.6 %copy-start.3 = (f32[32,1,128]{2,1,0:T(1,128)S(1)}, f32[32,1,128]{2,1,0:T(1,128)}, u32[]{:S(2)}) copy-start(f32[32,1,128]{2,1,0:T(1,128)} %get-tuple-element.17) | copy-start | bytes 49156
  98.8 0.7 copy-start.10
where the time goes:
time: 137 us; the launch traced here: 136 us
  Pallas kernels  64.3 us (47%)
  blocking collectives  45 us (33%)
  local copies, waits for them, and re-layouts  11.7 us (9%)
  starting transfers between devices  10.1 us (7%)
  other arithmetic  3.79 us (3%)
  between operations  1.5 us (1%)
    pallas_call x1, Pallas kernels, run_replica(): pl.pallas_call(replica_kernel, out_shape=(vec, vec, jax.ShapeDtypeStruct(...  64.3 us
    psum x1, blocking collectives, local_whole(): grad_coupling = lax.psum(part, 'rep')  21.3 us
    all_gather x1, blocking collectives, local_whole(): energies = lax.all_gather(en[0, 0:1], 'atom', axis=0, tiled=True)  12.3 us
    unnamed x35, local copies, waits for them, and re-layouts  7.23 us
    all_gather x1, blocking collectives, local_whole(): lax.all_gather(jnp.stack([interaction_strength, reciprocal_particle_weigh...  6.28 us
    all_gather x1, blocking collectives, local_whole(): slots = lax.all_gather(companion_group_indices, 'atom', axis=1, tiled=True)  5.17 us
    all_to_all x1, starting transfers between devices, local_whole(): mine = lax.all_to_all(packed, 'atom', 0, 0, tiled=True)  3.54 us
    all_to_all x1, starting transfers between devices, local_whole(): done = lax.all_to_all(done, 'atom', 0, 0, tiled=True)  3.54 us
  transfers between devices with their start and end apart: 3, of which 0 were waited for; matrix products, arithmetic and copies ran while one was open for 6% of the time, Pallas kernels for 0%

commit v1 on v0

--- a/solution.py
+++ b/solution.py
@@ -261,21 +261,42 @@
     fac_ref,
     cur_ref,
 ):
-    nb, _, width = x0_ref.shape
+    owners, _, atoms = x0_ref.shape
+    nb, _, width = f_ref.shape
+    blocks = nb // owners
     evals = rows_x.shape[0]
     steps = evals - 1
     partners = 2
     half = 0.5 * TIME_STEP
-    block_count = temp_ref[2]
+    block_count = blocks
     dof = float(3 * nb * width)
     f32, bf16 = jnp.float32, jnp.bfloat16
     real = slice(0, nb)
-    t_first = jnp.full((1, width), temp_ref[0], f32)
-    t_last = jnp.full((1, width), temp_ref[1], f32)
+    t_first = temp_ref[0:1]
+    t_last = temp_ref[1:2]
     swap_gain = jnp.sqrt(t_last / t_first)
     strength = 0.5 * block_count / (8.0 * partners)
-    log_scale = jnp.log(strength * jnp.ones((1, width), f32)) * LOG2E
-    mass = m_ref[...]
+    log_scale = math.log2(strength)
+
+    def whole(ref):
+        return jnp.stack(
+            [
+                ref[o, :, j * width : (j + 1) * width]
+                for o in range(owners)
+                for j in range(blocks)
+            ]
+        )
+
+    def give(ref, value):
+        for o in range(owners):
+            for j in range(blocks):
+                ref[o, :, j * width : (j + 1) * width] = value[o * blocks + j]
+
+    def far(n, p, k):
+        return far_ref[p // blocks, (n * blocks + p % blocks) * partners + k]
+
+    mass = whole(m_ref)
+    coupling = whole(c_ref)
 
     for ref in (left_w, right_w, rows_w):
         ref[...] = jnp.zeros_like(ref)
@@ -289,14 +310,12 @@
     zero_pad = (((0,), (0,)), ((), ()))
 
     def pair(ref, n, p):
-        base = (n * nb + p) * partners
-        return jnp.concatenate([ref[far_ref[base]], ref[far_ref[base + 1]]], axis=1)
+        return jnp.concatenate([ref[far(n, p, k)] for k in range(partners)], axis=1)
 
     def scatter(out, acc, n):
         for p in range(nb):
-            base = (n * nb + p) * partners
             for k in range(partners):
-                q = far_ref[base + k]
+                q = far(n, p, k)
                 acc[q] = acc[q] + out[p, :, k * width : (k + 1) * width]
 
     def set_rows(dest, value):
@@ -323,7 +342,7 @@
 
     def force(x, n):
         set_rows(rows_x.at[n], x)
-        self_term = -0.5 * LOG2E * row_sum(x * x) + jnp.log(c_ref[...]) * LOG2E
+        self_term = -0.5 * LOG2E * row_sum(x * x) + jnp.log(coupling) * LOG2E
         at = products(split3(x * LOG2E), split3(x), 0)
         at = singles(left_w, right_w, self_term + log_scale, at)
         at = singles(right_w, left_w, self_term, at)
@@ -405,7 +424,7 @@
         back_x = g * acc_w[real, 9:10, :] - pulled_w - x * total_v + pulled_v
         return back_x, total_v
 
-    x, v, goal = x0_ref[...], v0_ref[...], t_first
+    x, v, goal = whole(x0_ref), whole(v0_ref), t_first
     force(x, 0)
     for n in range(steps):
         if n == steps // 2:
@@ -422,21 +441,18 @@
         saved_u[n] = u
         fac_ref[n] = factor
         cur_ref[n] = current
-    xf_ref[...] = x
-    vf_ref[...] = v
-    coupling = c_ref[...]
+    give(xf_ref, x)
+    give(vf_ref, v)
     selfs = jnp.zeros((1, width), f32)
     square = strength * jnp.sum(coupling * coupling, axis=1)
-    owned = jnp.zeros((1, width), f32)
     for p in range(nb):
-        base = (steps * nb + p) * partners
         for k in range(partners):
-            hit = (far_ref[base + k] == p).astype(f32)
+            hit = (far(steps, p, k) == p).astype(f32)
             selfs = selfs + hit * square[p : p + 1]
     total = whole_sum(acc_w[real, 9:10, :]) * 0.5 - whole_sum(selfs)
     en_ref[...] = total / float(nb * width)
 
-    cot_x, cot_v = cx_ref[...], cv_ref[...]
+    cot_x, cot_v = whole(cx_ref), whole(cv_ref)
     cot_f = jnp.zeros_like(cot_x)
     cot_c = jnp.zeros((nb, 1, width), f32)
     for n in reversed(range(steps)):
@@ -454,15 +470,16 @@
         if n == steps // 2:
             cot_v = cot_v * swap_gain
     back_x, back_c = force_back(cot_f, 0)
-    gx_ref[...] = cot_x + back_x
-    gv_ref[...] = cot_v
-    gc_ref[...] = (cot_c + back_c) / coupling
-
-
-def run_replica(far, temps, x0, v0, cx, cv, coupling, mass, evals):
-    nb, _, width = x0.shape
+    give(gx_ref, cot_x + back_x)
+    give(gv_ref, cot_v)
+    give(gc_ref, (cot_c + back_c) / coupling)
+
+
+def run_replica(far, temps, x0, v0, cx, cv, coupling, mass, evals, blocks):
+    owners, _, atoms = x0.shape
+    nb, width = owners * blocks, atoms // blocks
     f32, bf16 = jnp.float32, jnp.bfloat16
-    vec = jax.ShapeDtypeStruct((nb, 3, width), f32)
+    vec = jax.ShapeDtypeStruct((owners, 3, atoms), f32)
     vmem = pl.BlockSpec(memory_space=pltpu.VMEM)
     smem = pl.BlockSpec(memory_space=pltpu.SMEM)
     return pl.pallas_call(
@@ -473,9 +490,9 @@
             jax.ShapeDtypeStruct((1, width), f32),
             vec,
             vec,
-            jax.ShapeDtypeStruct((nb, 1, width), f32),
+            jax.ShapeDtypeStruct((owners, 1, atoms), f32),
         ),
-        in_specs=[smem, smem] + [vmem] * 6,
+        in_specs=[smem] + [vmem] * 7,
         out_specs=[vmem] * 6,
         scratch_shapes=[
             pltpu.VMEM((nb, KCROSS, width), bf16),
@@ -499,6 +516,181 @@
     )(far, temps, x0, v0, cx, cv, coupling, mass)
 
 
+MESH = pl.DeviceIdType.MESH
+
+
+def greet(peers):
+    barrier = pltpu.get_barrier_semaphore()
+    for peer in peers:
+        pl.semaphore_signal(barrier, inc=1, device_id=peer, device_id_type=MESH)
+    pl.semaphore_wait(barrier, len(peers))
+
+
+def others(axis):
+    me, count = lax.axis_index(axis), lax.axis_size(axis)
+    return [lax.rem(me + d, count) for d in range(1, count)]
+
+
+def entry_kernel(blocks, partners, *refs):
+    ins, outs = refs[:9], refs[9:17]
+    heat_in, send_sem, recv_sem, heat_send, heat_recv = refs[17:]
+    split, shared = ins[:4], ins[4:7]
+    heat_ref, flag_ref = ins[7:]
+    temp_ref = outs[7]
+    me, owners = lax.axis_index("atom"), lax.axis_size("atom")
+    rep = lax.axis_index("rep")
+    partner = rep + 1 - 2 * lax.rem(rep, 2)
+    peers = others("atom")
+    twin = {"rep": partner, "atom": me}
+    greet([{"rep": rep, "atom": peer} for peer in peers] + [twin])
+    heat_copy = pltpu.make_async_remote_copy(
+        src_ref=heat_ref,
+        dst_ref=heat_in,
+        send_sem=heat_send,
+        recv_sem=heat_recv,
+        device_id=twin,
+        device_id_type=MESH,
+    )
+    heat_copy.start()
+    copies = []
+    for d, peer in enumerate(peers):
+        for i in range(7):
+            copies.append(
+                pltpu.make_async_remote_copy(
+                    src_ref=ins[i].at[peer] if i < 4 else ins[i],
+                    dst_ref=outs[i].at[me],
+                    send_sem=send_sem.at[d, i],
+                    recv_sem=recv_sem.at[d, i],
+                    device_id={"rep": rep, "atom": peer},
+                    device_id_type=MESH,
+                )
+            )
+            copies[-1].start()
+    for i in range(7):
+        outs[i][me] = ins[i][me] if i < 4 else ins[i][...]
+    heat_copy.wait()
+    own = heat_ref[...]
+    upcoming = jnp.where(flag_ref[...] == 1, heat_in[...], own)
+    lane = lax.broadcasted_iota(jnp.int32, own.shape, 1)
+    for row, value in enumerate((own, upcoming)):
+        chosen = jnp.sum(jnp.where(lane == me, value, 0.0), axis=1, keepdims=True)
+        temp_ref[row : row + 1, :] = jnp.broadcast_to(chosen, own.shape)
+    for copy in copies:
+        copy.wait()
+    slots = outs[6][...]
+    owner = lax.broadcasted_iota(jnp.int32, slots.shape, 0)
+    block = slots + (owner - 1) * blocks
+    inside = (block >= 0) & (block < owners * blocks)
+    outs[6][...] = jnp.where(inside, block, owners * blocks)
+
+
+def exit_kernel(*refs):
+    ins, outs = refs[:6], refs[6:12]
+    en_in, gc_in, rep_in, total, send_sem, recv_sem, rep_send, rep_recv = refs[12:]
+    en_ref, gc_ref = ins[4], ins[5]
+    me, rep = lax.axis_index("atom"), lax.axis_index("rep")
+    peers, rep_peers = others("atom"), others("rep")
+    greet(
+        [{"rep": rep, "atom": peer} for peer in peers]
+        + [{"rep": peer, "atom": me} for peer in rep_peers]
+    )
+    dests = (gc_in,) + tuple(outs[:4]) + (en_in,)
+    sources = (gc_ref,) + tuple(ins[:4]) + (en_ref,)
+    copies = {}
+    for i in range(6):
+        for d, peer in enumerate(peers):
+            copies[d, i] = pltpu.make_async_remote_copy(
+                src_ref=sources[i].at[peer] if i < 5 else sources[i],
+                dst_ref=dests[i].at[me] if i else gc_in.at[d],
+                send_sem=send_sem.at[d, i],
+                recv_sem=recv_sem.at[d, i],
+                device_id={"rep": rep, "atom": peer},
+                device_id_type=MESH,
+            )
+            copies[d, i].start()
+    part = gc_ref[me]
+    for d in range(len(peers)):
+        copies[d, 0].wait()
+        part = part + gc_in[d]
+    total[...] = part
+    rep_copies = []
+    for d, peer in enumerate(rep_peers):
+        rep_copies.append(
+            pltpu.make_async_remote_copy(
+                src_ref=total,
+                dst_ref=rep_in.at[d],
+                send_sem=rep_send.at[d],
+                recv_sem=rep_recv.at[d],
+                device_id={"rep": peer, "atom": me},
+                device_id_type=MESH,
+            )
+        )
+        rep_copies[-1].start()
+    for i in range(4):
+        outs[i][me] = ins[i][me]
+    en_in[me] = en_ref[...]
+    for d in range(len(peers)):
+        for i in range(1, 6):
+            copies[d, i].wait()
+    outs[4][...] = en_in[...]
+    for d, copy in enumerate(rep_copies):
+        copy.wait()
+        part = part + rep_in[d]
+    outs[5][...] = part
+
+
+def enter(split, shared, heat, flags, blocks, partners):
+    f32 = jnp.float32
+    owners = lax.axis_size("atom")
+    vmem = pl.BlockSpec(memory_space=pltpu.VMEM)
+    dma = pltpu.SemaphoreType.DMA
+    return pl.pallas_call(
+        functools.partial(entry_kernel, blocks, partners),
+        out_shape=tuple(jax.ShapeDtypeStruct(a.shape, f32) for a in split)
+        + tuple(jax.ShapeDtypeStruct((owners,) + a.shape, a.dtype) for a in shared)
+        + (jax.ShapeDtypeStruct((2, heat.shape[1]), f32),),
+        in_specs=[vmem] * 9,
+        out_specs=[vmem] * 8,
+        scratch_shapes=[
+            pltpu.VMEM(heat.shape, f32),
+            dma((owners - 1, 7)),
+            dma((owners - 1, 7)),
+            dma,
+            dma,
+        ],
+        compiler_params=pltpu.CompilerParams(collective_id=0, has_side_effects=True),
+    )(*split, *shared, heat, flags)
+
+
+def leave(xf, vf, gx, gv, en, gc):
+    f32 = jnp.float32
+    owners, reps = lax.axis_size("atom"), lax.axis_size("rep")
+    vmem = pl.BlockSpec(memory_space=pltpu.VMEM)
+    dma = pltpu.SemaphoreType.DMA
+    vec = jax.ShapeDtypeStruct(xf.shape, f32)
+    return pl.pallas_call(
+        exit_kernel,
+        out_shape=(vec, vec, vec, vec)
+        + (
+            jax.ShapeDtypeStruct((owners,) + en.shape, f32),
+            jax.ShapeDtypeStruct(gc.shape[1:], f32),
+        ),
+        in_specs=[vmem] * 6,
+        out_specs=[vmem] * 6,
+        scratch_shapes=[
+            pltpu.VMEM((owners,) + en.shape, f32),
+            pltpu.VMEM((owners - 1,) + gc.shape[1:], f32),
+            pltpu.VMEM((reps - 1,) + gc.shape[1:], f32),
+            pltpu.VMEM(gc.shape[1:], f32),
+            dma((owners - 1, 6)),
+            dma((owners - 1, 6)),
+            dma((reps - 1,)),
+            dma((reps - 1,)),
+        ],
+        compiler_params=pltpu.CompilerParams(collective_id=1, has_side_effects=True),
+    )(xf, vf, gx, gv, en, gc)
+
+
 def local_whole(
     starting_locations,
     starting_speeds,
@@ -511,63 +703,31 @@
     companion_group_indices,
 ):
     evals, blocks, partners = companion_group_indices.shape
-    owners = lax.axis_size("atom")
-    me = lax.axis_index("atom")
-    atoms = starting_locations.shape[2]
-    width = atoms // blocks
-    nb = owners * blocks
-    packed = jnp.concatenate(
-        [
-            starting_locations,
-            starting_speeds,
-            terminal_location_adjoint,
-            terminal_speed_adjoint,
-        ],
-        axis=1,
-    )
-    mine = lax.all_to_all(packed, "atom", 0, 0, tiled=True)
-    mine = mine.reshape(owners, 12, blocks, width).transpose(0, 2, 1, 3).reshape(nb, 12, width)
-    shared = lax.all_gather(
-        jnp.stack([interaction_strength, reciprocal_particle_weight]), "atom", axis=0
-    )
-    coupling = shared[:, 0].reshape(nb, 1, width)
-    mass = shared[:, 1].reshape(nb, 1, width)
-    slots = lax.all_gather(companion_group_indices, "atom", axis=1, tiled=True)
-    block_ids = jnp.arange(nb, dtype=jnp.int32)
-    far = (block_ids // blocks * blocks - blocks)[None, :, None] + slots
-    far = jnp.where((far >= 0) & (far < nb), far, nb).reshape(-1)
-    partner_temp = from_partner(heat_levels, "rep", 0)
-    upcoming = jnp.where(swap_indicator == 1, partner_temp, heat_levels)
-    temps = jnp.stack(
-        [
-            lax.dynamic_index_in_dim(heat_levels, me, keepdims=False),
-            lax.dynamic_index_in_dim(upcoming, me, keepdims=False),
-            jnp.float32(blocks),
-        ]
+    lanes = starting_locations.shape[2] // blocks
+
+    def row(x):
+        x = x.reshape(1, -1)
+        return jnp.pad(x, ((0, 0), (0, -x.shape[1] % lanes)))
+
+    *mine, coupling, mass, far, temps = enter(
+        (starting_locations, starting_speeds, terminal_location_adjoint, terminal_speed_adjoint),
+        (row(interaction_strength), row(reciprocal_particle_weight), row(companion_group_indices)),
+        row(heat_levels),
+        row(swap_indicator),
+        blocks,
+        partners,
     )
     xf, vf, en, gx, gv, gc = run_replica(
-        far,
-        temps,
-        mine[:, 0:3],
-        mine[:, 3:6],
-        mine[:, 6:9],
-        mine[:, 9:12],
-        coupling,
-        mass,
-        evals,
-    )
-    done = jnp.concatenate([xf, vf, gx, gv], axis=1)
-    done = done.reshape(owners, blocks, 12, width).transpose(0, 2, 1, 3).reshape(owners, 12, atoms)
-    done = lax.all_to_all(done, "atom", 0, 0, tiled=True)
-    energies = lax.all_gather(en[0, 0:1], "atom", axis=0, tiled=True)
-    part = lax.psum_scatter(gc.reshape(-1), "atom", scatter_dimension=0, tiled=True)
-    grad_coupling = lax.psum(part, "rep")
-    return (done[:, 0:3], done[:, 3:6], energies, done[:, 6:9], done[:, 9:12], grad_coupling)
+        far[:, 0], temps, *mine, coupling, mass, evals, blocks
+    )
+    xf, vf, gx, gv, energies, grad_coupling = leave(xf, vf, gx, gv, en, gc)
+    return (xf, vf, energies[:, 0, 0], gx, gv, grad_coupling.reshape(-1))
 
 
 def local(*args):
     partners = args[8].shape[2]
-    if args[0].shape[0] == lax.axis_size("atom") and partners == 2:
+    fits = args[0].shape[0] == lax.axis_size("atom") and partners == 2
+    if fits and lax.axis_size("rep") % 2 == 0:
         return local_whole(*args)
     return local_general(*args)
 

time: 137 us -> 98.4 us (0.72)
  blocking collectives: 45 us -> 0 us
  Pallas kernels: 64.3 us -> 86 us
  starting transfers between devices: 10.1 us -> 0 us
  other arithmetic: 3.79 us -> 0 us
    all_gather x3 -> x0, blocking collectives: 23.7 us -> none  [the longest x1 12.3 us: local_whole(): energies = lax.all_gather(en[0, 0:1], 'atom', axis=0, tiled=True)]
    pallas_call x0 -> x2, Pallas kernels: none -> 21.4 us  [the longest x1 11.9 us: leave(): pl.pallas_call(exit_kernel, out_shape=(vec, vec, vec, vec) + (jax.ShapeDt...]
    psum x1 -> x0, blocking collectives: 21.3 us -> none  [local_whole(): grad_coupling = lax.psum(part, 'rep')]
    all_to_all x2 -> x0, starting transfers between devices: 7.07 us -> none  [the longest x1 3.54 us: local_whole(): mine = lax.all_to_all(packed, 'atom', 0, 0, tiled=True)]
    ppermute x1 -> x0, starting transfers between devices: 3.03 us -> none  [from_partner(): lax.ppermute(x, axis, [(i, i ^ 1 << apart) for i in range(lax.axis_size(a...]
    pad x0 -> x3, local copies, waits for them, and re-layouts: none -> 2.88 us  [row(): return jnp.pad(x, ((0, 0), (0, -x.shape[1] % lanes)))]
    another operation x1 -> x0, other arithmetic: 1.88 us -> none  [local_whole(): jnp.stack([lax.dynamic_index_in_dim(heat_levels, me, keepdims=False), lax...]
    concatenate x2 -> x0, other arithmetic: 1.8 us -> none  [the longest x1 1.02 us: local_whole(): done = jnp.concatenate([xf, vf, gx, gv], axis=1)]
  transfers between devices with their start and end apart: 3 -> 0, of which waited for: 0 -> 0; matrix products, arithmetic and copies ran while one was open for 6% -> 0% of each run, Pallas kernels for 0% -> 0%
where the time goes in v1:
time: 98.4 us; the launch traced here: 97.8 us
  Pallas kernels  86 us (87%)
  local copies, waits for them, and re-layouts  11.1 us (11%)
    pallas_call x1, Pallas kernels, run_replica(): pl.pallas_call(replica_kernel, out_shape=(vec, vec, jax.ShapeDtypeStruct(...  64.6 us
    pallas_call x1, Pallas kernels, leave(): pl.pallas_call(exit_kernel, out_shape=(vec, vec, vec, vec) + (jax.ShapeDt...  11.9 us
    pallas_call x1, Pallas kernels, enter(): pl.pallas_call(functools.partial(entry_kernel, blocks, partners), out_sha...  9.49 us
    unnamed x30, local copies, waits for them, and re-layouts  7.47 us
    pad x3, local copies, waits for them, and re-layouts, row(): return jnp.pad(x, ((0, 0), (0, -x.shape[1] % lanes)))  2.88 us

profile of v1, /device:TPU:0, one launch (start us, length us, event | category | flops | bytes accessed | tf_op | source)
XLA Modules:
  0.0 97.8 jit_solution(16878870486623831360)
XLA Ops:
  0.7 1.2 %pad.13.refs_7_ = f32[1,128]{1,0:T(1,128)} pad(f32[1,4]{1,0:T(1,128)} %bitcast.10, f32[]{:T(128)} %constant.3.clone.1), padding=0_0x0_124 | pad | bytes 532 | tf_op jit(solution)/shard_map/jit(_pad)/pad | solution.py:710
  1.8 1.2 %pad.14.refs_8_ = s32[1,128]{1,0:T(1,128)} pad(s32[1,4]{1,0:T(1,128)} %bitcast.11, s32[]{:T(128)} %constant.2.clone.1), padding=0_0x0_124 | pad | bytes 532 | tf_op jit(solution)/shard_map/jit(_pad)/pad | solution.py:710
  3.0 0.0 copy-done.7
  3.0 0.1 copy.24
  3.1 0.1 reshape.32
  3.2 0.5 pad.12.refs_6_
  3.8 0.7 copy.25.refs_0_
  4.4 0.1 copy-done.4
  4.6 0.7 copy.26.refs_1_
  5.2 0.1 copy-done.5
  5.4 0.7 copy.27.refs_2_
  6.0 0.1 copy-done.6
  6.2 0.7 copy.28.refs_3_
  6.8 9.5 %shard_map.136 = (f32[4,3,1024]{2,1,0:T(4,128)}, f32[4,3,1024]{2,1,0:T(4,128)}, f32[4,3,1024]{2,1,0:T(4,128)}, f32[4,3,1024]{2,1,0:T(4,128)}, f32[4,1,1024]{2,1,...) custom-call(f32[4,3,1024]{2,1,0:T(4,128)} %copy.25.refs_0_, ...), custom_call_target="tpu_custom_call" | custom-call | tf_op jit(solution)/shard_map/pallas_call | solution.py:647
  16.3 64.6 %shard_map.137 = (f32[4,3,1024]{2,1,0:T(4,128)}, f32[4,3,1024]{2,1,0:T(4,128)}, f32[1,128]{1,0:T(1,128)}, f32[4,3,1024]{2,1,0:T(4,128)}, f32[4,3,1024]{2,1,0:T(4,128)}, /*index=5*/f32[4,1,1024]{2,1,0:T(1,128)}) custom-call(s32[4,128]{1,0:T(4,128)} %bitcast.9, f32[2,128]{1,0:T(2,128)} %get-tuple-element.27.temp_ref, f32[4,3,1024]{2,1,0:T(4,128)} %get-tuple-element.28.x0_ref, ...), custom_call_target="tpu_custom_call" | custom-call | tf_op jit(solution)/shard_map/pallas_call | solution.py:485
  80.9 11.9 %shard_map.138 = (f32[4,3,1024]{2,1,0:T(4,128)}, f32[4,3,1024]{2,1,0:T(4,128)}, f32[4,3,1024]{2,1,0:T(4,128)}, f32[4,3,1024]{2,1,0:T(4,128)}, f32[4,1,128]{2,1,0:T(1,128)}, /*index=5*/f32[1,1024]{1,0:T(1,128)}) custom-call(f32[4,3,1024]{2,1,0:T(4,128)} %get-tuple-element.34.refs_0_, f32[4,3,1024]{2,1,0:T(4,128)} %get-tuple-element.35.refs_1_, ...), custom_call_target="tpu_custom_call" | custom-call | tf_op jit(solution)/shard_map/pallas_call | solution.py:671
  92.9 1.5 %copy.29 = f32[4,3,1024]{2,0,1:T(4,128)} copy(f32[4,3,1024]{2,1,0:T(4,128)} %get-tuple-element.52) | data formatting | bytes 98304
  94.4 0.6 slice_reduce_fusion
  95.0 0.7 copy.30
  95.7 0.7 copy.31
  96.3 0.2 copy-done
  96.5 0.7 copy.32
  97.2 0.0 copy-done.8
  97.2 0.6 copy.34
  (14 shorter events, 0.0 us)
Async XLA Ops:
  0.6 2.4 %copy-start.7 = (s32[5,8,2]{1,2,0:T(2,128)S(1)}, s32[5,8,2]{1,2,0:T(2,128)}, u32[]{:S(2)}) copy-start(s32[5,8,2]{1,2,0:T(2,128)} %param.17) | copy-start | bytes 964
  0.6 3.1 %copy-start.3 = (f32[4,3,1024]{2,0,1:T(4,128)S(1)}, f32[4,3,1024]{2,0,1:T(4,128)}, u32[]{:S(2)}) copy-start(f32[4,3,1024]{2,0,1:T(4,128)} %param.9) | copy-start | bytes 147460
  3.8 0.8 copy-start.4
  4.6 0.8 copy-start.5
  5.4 0.8 copy-start.6
  92.9 2.2 %copy-start.2 = (f32[4,3,1024]{2,1,0:T(4,128)S(1)}, f32[4,3,1024]{2,1,0:T(4,128)}, u32[]{:S(2)}) copy-start(f32[4,3,1024]{2,1,0:T(4,128)} %get-tuple-element.53) | copy-start | bytes 147460
  92.9 1.5 %copy-start.9 = (f32[4,1,128]{2,1,0:T(1,128)S(1)}, f32[4,1,128]{2,1,0:T(1,128)}, u32[]{:S(2)}) copy-start(f32[4,1,128]{2,1,0:T(1,128)} %get-tuple-element.42) | copy-start | bytes 6148
  94.4 1.3 %copy-start.1 = (f32[4,3,1024]{2,1,0:T(4,128)S(1)}, f32[4,3,1024]{2,1,0:T(4,128)}, u32[]{:S(2)}) copy-start(f32[4,3,1024]{2,1,0:T(4,128)} %get-tuple-element.55) | copy-start | bytes 147460
  95.7 0.8 copy-start
  96.5 0.7 copy-start.8

commit v2 on v1

--- a/solution.py
+++ b/solution.py
@@ -208,17 +208,15 @@
 
 LOG2E = math.log2(math.e)
 ROWS = 16
-KDIST = 32
-KCROSS = 48
-UNROLL = 4
-
-
-def split3(x):
+KDIST = 16
+KCROSS = 32
+KEPT = 8
+UNROLL = 8
+
+
+def split2(x):
     hi = x.astype(jnp.bfloat16).astype(jnp.float32)
-    rest = x - hi
-    mid = rest.astype(jnp.bfloat16).astype(jnp.float32)
-    low = (rest - mid).astype(jnp.bfloat16).astype(jnp.float32)
-    return hi, mid, low
+    return hi, (x - hi).astype(jnp.bfloat16).astype(jnp.float32)
 
 
 def row_sum(x):
@@ -257,6 +255,7 @@
     out_w,
     out_v,
     saved_u,
+    saved_x,
     f_ref,
     fac_ref,
     cur_ref,
@@ -293,7 +292,7 @@
                 ref[o, :, j * width : (j + 1) * width] = value[o * blocks + j]
 
     def far(n, p, k):
-        return far_ref[p // blocks, (n * blocks + p % blocks) * partners + k]
+        return far_ref[p // blocks, n, k, p % blocks]
 
     mass = whole(m_ref)
     coupling = whole(c_ref)
@@ -319,22 +318,21 @@
                 acc[q] = acc[q] + out[p, :, k * width : (k + 1) * width]
 
     def set_rows(dest, value):
-        hi, mid, low = split3(value)
+        hi, low = split2(value)
         put(rows_w, 0, hi)
-        put(rows_w, 3, mid)
-        put(rows_w, 6, low)
-        put(rows_w, 9, one)
+        put(rows_w, 3, low)
+        put(rows_w, 6, one)
         dest[...] = rows_w[...].astype(bf16)
 
     def products(first, second, at):
-        for i, j in ((0, 0), (0, 1), (1, 0), (0, 2), (1, 1), (2, 0)):
+        for i, j in ((0, 0), (0, 1), (1, 0)):
             put(left_w, at, first[i])
             put(right_w, at, second[j])
             at += first[0].shape[1]
         return at
 
     def singles(ref, other, value, at):
-        for part in split3(value):
+        for part in split2(value):
             put(ref, at, part)
             put(other, at, one)
             at += 1
@@ -342,11 +340,12 @@
 
     def force(x, n):
         set_rows(rows_x.at[n], x)
+        saved_x[n] = x
         self_term = -0.5 * LOG2E * row_sum(x * x) + jnp.log(coupling) * LOG2E
-        at = products(split3(x * LOG2E), split3(x), 0)
+        at = products(split2(x * LOG2E), split2(x), 0)
         at = singles(left_w, right_w, self_term + log_scale, at)
         at = singles(right_w, left_w, self_term, at)
-        right_w[nb, at - 3 : at - 2, :] = jnp.full((1, width), -1e6, f32)
+        right_w[nb, at - 2 : at - 1, :] = jnp.full((1, width), -1e6, f32)
         left[:, 0:KDIST, :] = left_w[real, 0:KDIST, :].astype(bf16)
         right[:, 0:KDIST, :] = right_w[:, 0:KDIST, :].astype(bf16)
 
@@ -362,26 +361,22 @@
                 )
                 w = jnp.exp2(exponent).astype(bf16)
                 weights[n, p] = w
-                out_w[p] = jnp.dot(rows_x[n, p], w, preferred_element_type=f32)
+                out_w[p] = jnp.dot(rows_x[n, p], w, preferred_element_type=f32)[:KEPT]
                 acc_w[p] = lax.dot_general(
                     pair(rows_x.at[n], n, p),
                     w,
                     (((1,), (1,)), ((), ())),
                     preferred_element_type=f32,
-                )
+                )[:KEPT]
 
         scatter(out_w, acc_w, n)
-        pulled = acc_w[real, 0:3, :] + acc_w[real, 3:6, :] + acc_w[real, 6:9, :]
-        f_ref[...] = x * acc_w[real, 9:10, :] - pulled
+        pulled = acc_w[real, 0:3, :] + acc_w[real, 3:6, :]
+        f_ref[...] = x * acc_w[real, 6:7, :] - pulled
 
     def force_back(g, n):
-        x = (
-            rows_x[n, real].astype(f32)[:, 0:3]
-            + rows_x[n, real].astype(f32)[:, 3:6]
-            + rows_x[n, real].astype(f32)[:, 6:9]
-        )
+        x = saved_x[n]
         set_rows(rows_g, g)
-        sx, sg = split3(x), split3(g)
+        sx, sg = split2(x), split2(g)
         neg_g = tuple(-part for part in sg)
         neg_x = tuple(-part for part in sx)
         at = products(sx, neg_g, 0)
@@ -401,27 +396,27 @@
                 )
                 w = weights[n, p]
                 v = (w.astype(f32) * phi).astype(bf16)
-                out_w[p] = jnp.dot(rows_g[p], w, preferred_element_type=f32)
-                out_v[p] = jnp.dot(rows_x[n, p], v, preferred_element_type=f32)
+                out_w[p] = jnp.dot(rows_g[p], w, preferred_element_type=f32)[:KEPT]
+                out_v[p] = jnp.dot(rows_x[n, p], v, preferred_element_type=f32)[:KEPT]
                 acc_w[p] = lax.dot_general(
                     pair(rows_g, n, p),
                     w,
                     (((1,), (1,)), ((), ())),
                     preferred_element_type=f32,
-                )
+                )[:KEPT]
                 acc_v[p] = lax.dot_general(
                     pair(rows_x.at[n], n, p),
                     v,
                     (((1,), (1,)), ((), ())),
                     preferred_element_type=f32,
-                )
+                )[:KEPT]
 
         scatter(out_w, acc_w, n)
         scatter(out_v, acc_v, n)
-        pulled_w = acc_w[real, 0:3, :] + acc_w[real, 3:6, :] + acc_w[real, 6:9, :]
-        pulled_v = acc_v[real, 0:3, :] + acc_v[real, 3:6, :] + acc_v[real, 6:9, :]
-        total_v = acc_v[real, 9:10, :]
-        back_x = g * acc_w[real, 9:10, :] - pulled_w - x * total_v + pulled_v
+        pulled_w = acc_w[real, 0:3, :] + acc_w[real, 3:6, :]
+        pulled_v = acc_v[real, 0:3, :] + acc_v[real, 3:6, :]
+        total_v = acc_v[real, 6:7, :]
+        back_x = g * acc_w[real, 6:7, :] - pulled_w - x * total_v + pulled_v
         return back_x, total_v
 
     x, v, goal = whole(x0_ref), whole(v0_ref), t_first
@@ -449,7 +444,7 @@
         for k in range(partners):
             hit = (far(steps, p, k) == p).astype(f32)
             selfs = selfs + hit * square[p : p + 1]
-    total = whole_sum(acc_w[real, 9:10, :]) * 0.5 - whole_sum(selfs)
+    total = whole_sum(acc_w[real, 6:7, :]) * 0.5 - whole_sum(selfs)
     en_ref[...] = total / float(nb * width)
 
     cot_x, cot_v = whole(cx_ref), whole(cv_ref)
@@ -503,11 +498,12 @@
             pltpu.VMEM((evals, nb + 1, ROWS, width), bf16),
             pltpu.VMEM((nb + 1, ROWS, width), bf16),
             pltpu.VMEM((evals, nb, width, 2 * width), bf16),
-            pltpu.VMEM((nb + 1, ROWS, width), f32),
-            pltpu.VMEM((nb + 1, ROWS, width), f32),
-            pltpu.VMEM((nb, ROWS, 2 * width), f32),
-            pltpu.VMEM((nb, ROWS, 2 * width), f32),
+            pltpu.VMEM((nb + 1, KEPT, width), f32),
+            pltpu.VMEM((nb + 1, KEPT, width), f32),
+            pltpu.VMEM((nb, KEPT, 2 * width), f32),
+            pltpu.VMEM((nb, KEPT, 2 * width), f32),
             pltpu.VMEM((evals - 1, nb, 3, width), f32),
+            pltpu.VMEM((evals, nb, 3, width), f32),
             pltpu.VMEM((nb, 3, width), f32),
             pltpu.VMEM((evals - 1, 1, width), f32),
             pltpu.VMEM((evals - 1, 1, width), f32),
@@ -533,14 +529,17 @@
 
 def entry_kernel(blocks, partners, *refs):
     ins, outs = refs[:9], refs[9:17]
-    heat_in, send_sem, recv_sem, heat_send, heat_recv = refs[17:]
-    split, shared = ins[:4], ins[4:7]
+    stage = refs[17:21]
+    heat_in, send_sem, recv_sem, heat_send, heat_recv = refs[21:]
     heat_ref, flag_ref = ins[7:]
     temp_ref = outs[7]
     me, owners = lax.axis_index("atom"), lax.axis_size("atom")
     rep = lax.axis_index("rep")
     partner = rep + 1 - 2 * lax.rem(rep, 2)
     peers = others("atom")
+    for i in range(4):
+        for r in range(owners):
+            stage[i][r] = ins[i][:, r, :]
     twin = {"rep": partner, "atom": me}
     greet([{"rep": rep, "atom": peer} for peer in peers] + [twin])
     heat_copy = pltpu.make_async_remote_copy(
@@ -557,7 +556,7 @@
         for i in range(7):
             copies.append(
                 pltpu.make_async_remote_copy(
-                    src_ref=ins[i].at[peer] if i < 4 else ins[i],
+                    src_ref=stage[i].at[peer] if i < 4 else ins[i],
                     dst_ref=outs[i].at[me],
                     send_sem=send_sem.at[d, i],
                     recv_sem=recv_sem.at[d, i],
@@ -567,14 +566,14 @@
             )
             copies[-1].start()
     for i in range(7):
-        outs[i][me] = ins[i][me] if i < 4 else ins[i][...]
+        outs[i][me] = stage[i][me] if i < 4 else ins[i][...]
     heat_copy.wait()
     own = heat_ref[...]
     upcoming = jnp.where(flag_ref[...] == 1, heat_in[...], own)
     lane = lax.broadcasted_iota(jnp.int32, own.shape, 1)
     for row, value in enumerate((own, upcoming)):
         chosen = jnp.sum(jnp.where(lane == me, value, 0.0), axis=1, keepdims=True)
-        temp_ref[row : row + 1, :] = jnp.broadcast_to(chosen, own.shape)
+        temp_ref[row : row + 1, :] = jnp.broadcast_to(chosen, (1, temp_ref.shape[1]))
     for copy in copies:
         copy.wait()
     slots = outs[6][...]
@@ -586,7 +585,8 @@
 
 def exit_kernel(*refs):
     ins, outs = refs[:6], refs[6:12]
-    en_in, gc_in, rep_in, total, send_sem, recv_sem, rep_send, rep_recv = refs[12:]
+    land = refs[12:16]
+    en_in, gc_in, rep_in, total, send_sem, recv_sem, rep_send, rep_recv = refs[16:]
     en_ref, gc_ref = ins[4], ins[5]
     me, rep = lax.axis_index("atom"), lax.axis_index("rep")
     peers, rep_peers = others("atom"), others("rep")
@@ -594,7 +594,7 @@
         [{"rep": rep, "atom": peer} for peer in peers]
         + [{"rep": peer, "atom": me} for peer in rep_peers]
     )
-    dests = (gc_in,) + tuple(outs[:4]) + (en_in,)
+    dests = (gc_in,) + tuple(land) + (en_in,)
     sources = (gc_ref,) + tuple(ins[:4]) + (en_ref,)
     copies = {}
     for i in range(6):
@@ -627,31 +627,40 @@
         )
         rep_copies[-1].start()
     for i in range(4):
-        outs[i][me] = ins[i][me]
+        land[i][me] = ins[i][me]
     en_in[me] = en_ref[...]
     for d in range(len(peers)):
         for i in range(1, 6):
             copies[d, i].wait()
-    outs[4][...] = en_in[...]
+    for i in range(4):
+        for r in range(lax.axis_size("atom")):
+            outs[i][:, r, :] = land[i][r]
+    lane = lax.broadcasted_iota(jnp.int32, en_ref.shape, 1)
+    energies = jnp.zeros(en_ref.shape, jnp.float32)
+    for r in range(lax.axis_size("atom")):
+        energies = jnp.where(lane == r, en_in[r], energies)
+    outs[4][...] = energies[:, : outs[4].shape[1]]
     for d, copy in enumerate(rep_copies):
         copy.wait()
         part = part + rep_in[d]
     outs[5][...] = part
 
 
-def enter(split, shared, heat, flags, blocks, partners):
+def enter(split, shared, heat, flags, blocks, partners, lanes):
     f32 = jnp.float32
+    moved = [(a.shape[1], a.shape[0], a.shape[2]) for a in split]
     owners = lax.axis_size("atom")
     vmem = pl.BlockSpec(memory_space=pltpu.VMEM)
     dma = pltpu.SemaphoreType.DMA
     return pl.pallas_call(
         functools.partial(entry_kernel, blocks, partners),
-        out_shape=tuple(jax.ShapeDtypeStruct(a.shape, f32) for a in split)
+        out_shape=tuple(jax.ShapeDtypeStruct(s, f32) for s in moved)
         + tuple(jax.ShapeDtypeStruct((owners,) + a.shape, a.dtype) for a in shared)
-        + (jax.ShapeDtypeStruct((2, heat.shape[1]), f32),),
+        + (jax.ShapeDtypeStruct((2, lanes), f32),),
         in_specs=[vmem] * 9,
         out_specs=[vmem] * 8,
-        scratch_shapes=[
+        scratch_shapes=[pltpu.VMEM(s, f32) for s in moved]
+        + [
             pltpu.VMEM(heat.shape, f32),
             dma((owners - 1, 7)),
             dma((owners - 1, 7)),
@@ -667,17 +676,18 @@
     owners, reps = lax.axis_size("atom"), lax.axis_size("rep")
     vmem = pl.BlockSpec(memory_space=pltpu.VMEM)
     dma = pltpu.SemaphoreType.DMA
-    vec = jax.ShapeDtypeStruct(xf.shape, f32)
+    vec = jax.ShapeDtypeStruct((xf.shape[1], owners, xf.shape[2]), f32)
     return pl.pallas_call(
         exit_kernel,
         out_shape=(vec, vec, vec, vec)
         + (
-            jax.ShapeDtypeStruct((owners,) + en.shape, f32),
+            jax.ShapeDtypeStruct((1, owners), f32),
             jax.ShapeDtypeStruct(gc.shape[1:], f32),
         ),
         in_specs=[vmem] * 6,
         out_specs=[vmem] * 6,
-        scratch_shapes=[
+        scratch_shapes=[pltpu.VMEM(xf.shape, f32)] * 4
+        + [
             pltpu.VMEM((owners,) + en.shape, f32),
             pltpu.VMEM((owners - 1,) + gc.shape[1:], f32),
             pltpu.VMEM((reps - 1,) + gc.shape[1:], f32),
@@ -705,23 +715,42 @@
     evals, blocks, partners = companion_group_indices.shape
     lanes = starting_locations.shape[2] // blocks
 
-    def row(x):
-        x = x.reshape(1, -1)
-        return jnp.pad(x, ((0, 0), (0, -x.shape[1] % lanes)))
+    def turned(x):
+        return x.transpose(1, 0, 2)
 
     *mine, coupling, mass, far, temps = enter(
-        (starting_locations, starting_speeds, terminal_location_adjoint, terminal_speed_adjoint),
-        (row(interaction_strength), row(reciprocal_particle_weight), row(companion_group_indices)),
-        row(heat_levels),
-        row(swap_indicator),
+        tuple(
+            turned(x)
+            for x in (
+                starting_locations,
+                starting_speeds,
+                terminal_location_adjoint,
+                terminal_speed_adjoint,
+            )
+        ),
+        (
+            interaction_strength.reshape(1, -1),
+            reciprocal_particle_weight.reshape(1, -1),
+            companion_group_indices.transpose(0, 2, 1),
+        ),
+        heat_levels.reshape(1, -1),
+        swap_indicator.reshape(1, -1),
         blocks,
         partners,
+        lanes,
     )
     xf, vf, en, gx, gv, gc = run_replica(
-        far[:, 0], temps, *mine, coupling, mass, evals, blocks
+        far, temps, *mine, coupling, mass, evals, blocks
     )
     xf, vf, gx, gv, energies, grad_coupling = leave(xf, vf, gx, gv, en, gc)
-    return (xf, vf, energies[:, 0, 0], gx, gv, grad_coupling.reshape(-1))
+    return (
+        turned(xf),
+        turned(vf),
+        energies[0],
+        turned(gx),
+        turned(gv),
+        grad_coupling.reshape(-1),
+    )
 
 
 def local(*args):

time: 98.4 us -> 96.4 us (0.980)
  local copies, waits for them, and re-layouts: 11.1 us -> 4.71 us
  Pallas kernels: 86 us -> 90.5 us
    pallas_call x1, Pallas kernels: 64.6 us -> 69 us  [run_replica(): pl.pallas_call(replica_kernel, out_shape=(vec, vec, jax.ShapeDtypeStruct(...]
    pad x3 -> x0, local copies, waits for them, and re-layouts: 2.88 us -> none  [row(): return jnp.pad(x, ((0, 0), (0, -x.shape[1] % lanes)))]
    unnamed x30 -> x16, local copies, waits for them, and re-layouts: 7.47 us -> 4.71 us
where the time goes in v2:
time: 96.4 us; the launch traced here: 95.9 us
  Pallas kernels  90.5 us (94%)
  local copies, waits for them, and re-layouts  4.71 us (5%)
    pallas_call x1, Pallas kernels, run_replica(): pl.pallas_call(replica_kernel, out_shape=(vec, vec, jax.ShapeDtypeStruct(...  69 us
    pallas_call x1, Pallas kernels, leave(): pl.pallas_call(exit_kernel, out_shape=(vec, vec, vec, vec) + (jax.ShapeDt...  12 us
    pallas_call x1, Pallas kernels, enter(): pl.pallas_call(functools.partial(entry_kernel, blocks, partners), out_sha...  9.56 us
    unnamed x16, local copies, waits for them, and re-layouts  4.71 us

profile of v2, /device:TPU:0, one launch (start us, length us, event | category | flops | bytes accessed | tf_op | source)
XLA Modules:
  0.0 95.9 jit_solution(10787184907204459548)
XLA Ops:
  0.6 9.6 %shard_map.136 = (f32[4,3,1024]{2,1,0:T(4,128)}, f32[4,3,1024]{2,1,0:T(4,128)}, f32[4,3,1024]{2,1,0:T(4,128)}, f32[4,3,1024]{2,1,0:T(4,128)}, f32[4,1,1024]{2,1,...) custom-call(f32[3,4,1024]{2,1,0:T(4,128)} %bitcast.19, f32[3,4,1024]{2,1,0:T(4,128)} %bitcast.20, ...), custom_call_target="tpu_custom_call" | custom-call | tf_op jit(solution)/shard_map/pallas_call | solution.py:655
  10.2 69.0 %shard_map.137 = (f32[4,3,1024]{2,1,0:T(4,128)}, f32[4,3,1024]{2,1,0:T(4,128)}, f32[1,128]{1,0:T(1,128)}, f32[4,3,1024]{2,1,0:T(4,128)}, f32[4,3,1024]{2,1,0:T(4,128)}, /*index=5*/f32[4,1,1024]{2,1,0:T(1,128)}) custom-call(s32[4,5,2,8]{3,2,1,0:T(2,128)} %get-tuple-element.26.far_ref, f32[2,128]{1,0:T(2,128)} %get-tuple-element.27.temp_ref, ...), custom_call_target="tpu_custom_call" | custom-call | tf_op jit(solution)/shard_map/pallas_call | solution.py:480
  79.2 12.0 %shard_map.138 = (f32[3,4,1024]{2,1,0:T(4,128)}, f32[3,4,1024]{2,1,0:T(4,128)}, f32[3,4,1024]{2,1,0:T(4,128)}, f32[3,4,1024]{2,1,0:T(4,128)}, f32[1,4]{1,0:T(1,128)}, /*index=5*/f32[1,1024]{1,0:T(1,128)}) custom-call(f32[4,3,1024]{2,1,0:T(4,128)} %get-tuple-element.34.refs_0_, f32[4,3,1024]{2,1,0:T(4,128)} %get-tuple-element.35.refs_1_, ...), custom_call_target="tpu_custom_call" | custom-call | tf_op jit(solution)/shard_map/pallas_call | solution.py:680
  91.2 0.0 copy-start.2
  91.2 1.4 %copy.21 = f32[4,3,1024]{2,0,1:T(4,128)} copy(f32[4,3,1024]{2,0,1:T(4,128)} %bitcast.18) | data formatting | bytes 98304
  92.6 0.0 copy-done.2
  92.6 0.0 copy-start.4
  92.6 0.0 copy-start.1
  92.6 0.6 copy.22
  93.2 0.0 copy-done.4
  93.3 0.5 copy.23
  93.8 0.0 copy-done.1
  93.8 0.0 copy-start
  93.8 0.6 copy.24
  94.4 0.2 copy-done
  94.6 0.0 copy-start.3
  94.6 0.6 copy.25
  95.2 0.1 copy-done.3
  95.3 0.6 copy.26
Async XLA Ops:
  91.2 1.4 %copy-start.2 = (f32[3,4,1024]{2,1,0:T(4,128)S(1)}, f32[3,4,1024]{2,1,0:T(4,128)}, u32[]{:S(2)}) copy-start(f32[3,4,1024]{2,1,0:T(4,128)} %get-tuple-element.41) | copy-start | bytes 147460
  92.6 0.7 copy-start.4
  92.6 1.2 %copy-start.1 = (f32[3,4,1024]{2,1,0:T(4,128)S(1)}, f32[3,4,1024]{2,1,0:T(4,128)}, u32[]{:S(2)}) copy-start(f32[3,4,1024]{2,1,0:T(4,128)} %get-tuple-element.43) | copy-start | bytes 147460
  93.8 0.8 copy-start
  94.6 0.7 copy-start.3

commit v3 on v2

--- a/solution.py
+++ b/solution.py
@@ -292,7 +292,7 @@
                 ref[o, :, j * width : (j + 1) * width] = value[o * blocks + j]
 
     def far(n, p, k):
-        return far_ref[p // blocks, n, k, p % blocks]
+        return far_ref[p // blocks, (n * partners + k) * blocks + p % blocks]
 
     mass = whole(m_ref)
     coupling = whole(c_ref)
@@ -740,7 +740,7 @@
         lanes,
     )
     xf, vf, en, gx, gv, gc = run_replica(
-        far, temps, *mine, coupling, mass, evals, blocks
+        far.reshape(far.shape[0], -1), temps, *mine, coupling, mass, evals, blocks
     )
     xf, vf, gx, gv, energies, grad_coupling = leave(xf, vf, gx, gv, en, gc)
     return (

time: 96.4 us -> 97.3 us (level)
  local copies, waits for them, and re-layouts: 4.71 us -> 6.1 us
    reshape x0 -> x1, local copies, waits for them, and re-layouts: none -> 1.4 us  [local_whole(): far.reshape(far.shape[0], -1)]
where the time goes in v3:
time: 97.3 us; the launch traced here: 96.8 us
  Pallas kernels  90 us (92%)
  local copies, waits for them, and re-layouts  6.1 us (6%)
    pallas_call x1, Pallas kernels, run_replica(): pl.pallas_call(replica_kernel, out_shape=(vec, vec, jax.ShapeDtypeStruct(...  68.4 us
    pallas_call x1, Pallas kernels, leave(): pl.pallas_call(exit_kernel, out_shape=(vec, vec, vec, vec) + (jax.ShapeDt...  12 us
    pallas_call x1, Pallas kernels, enter(): pl.pallas_call(functools.partial(entry_kernel, blocks, partners), out_sha...  9.58 us
    unnamed x16, local copies, waits for them, and re-layouts  4.71 us

profile of v3, /device:TPU:0, one launch (start us, length us, event | category | flops | bytes accessed | tf_op | source)
XLA Modules:
  0.0 96.8 jit_solution(9854470635758372930)
XLA Ops:
  0.6 9.6 %shard_map.136 = (f32[4,3,1024]{2,1,0:T(4,128)}, f32[4,3,1024]{2,1,0:T(4,128)}, f32[4,3,1024]{2,1,0:T(4,128)}, f32[4,3,1024]{2,1,0:T(4,128)}, f32[4,1,1024]{2,1,...) custom-call(f32[3,4,1024]{2,1,0:T(4,128)} %bitcast.19, f32[3,4,1024]{2,1,0:T(4,128)} %bitcast.20, ...), custom_call_target="tpu_custom_call" | custom-call | tf_op jit(solution)/shard_map/pallas_call | solution.py:655
  10.2 1.4 %reshape.34.far_ref = s32[4,80]{1,0:T(4,128)} reshape(s32[4,5,2,8]{3,2,1,0:T(2,128)} %get-tuple-element.26) | data formatting | bytes 2560 | tf_op jit(solution)/shard_map/reshape | solution.py:743
  11.6 68.4 %shard_map.137 = (f32[4,3,1024]{2,1,0:T(4,128)}, f32[4,3,1024]{2,1,0:T(4,128)}, f32[1,128]{1,0:T(1,128)}, f32[4,3,1024]{2,1,0:T(4,128)}, f32[4,3,1024]{2,1,0:T(4,128)}, /*index=5*/f32[4,1,1024]{2,1,0:T(1,128)}) custom-call(s32[4,80]{1,0:T(4,128)} %reshape.34.far_ref, f32[2,128]{1,0:T(2,128)} %get-tuple-element.27.temp_ref, ...), custom_call_target="tpu_custom_call" | custom-call | tf_op jit(solution)/shard_map/pallas_call | solution.py:480
  80.1 12.0 %shard_map.138 = (f32[3,4,1024]{2,1,0:T(4,128)}, f32[3,4,1024]{2,1,0:T(4,128)}, f32[3,4,1024]{2,1,0:T(4,128)}, f32[3,4,1024]{2,1,0:T(4,128)}, f32[1,4]{1,0:T(1,128)}, /*index=5*/f32[1,1024]{1,0:T(1,128)}) custom-call(f32[4,3,1024]{2,1,0:T(4,128)} %get-tuple-element.34.refs_0_, f32[4,3,1024]{2,1,0:T(4,128)} %get-tuple-element.35.refs_1_, ...), custom_call_target="tpu_custom_call" | custom-call | tf_op jit(solution)/shard_map/pallas_call | solution.py:680
  92.0 0.0 copy-start.2
  92.1 1.4 %copy.21 = f32[4,3,1024]{2,0,1:T(4,128)} copy(f32[4,3,1024]{2,0,1:T(4,128)} %bitcast.18) | data formatting | bytes 98304
  93.5 0.0 copy-done.2
  93.5 0.0 copy-start.4
  93.5 0.0 copy-start.1
  93.5 0.6 copy.22
  94.1 0.0 copy-done.4
  94.2 0.5 copy.23
  94.7 0.0 copy-done.1
  94.7 0.0 copy-start
  94.7 0.6 copy.24
  95.3 0.2 copy-done
  95.5 0.0 copy-start.3
  95.5 0.6 copy.25
  96.1 0.1 copy-done.3
  96.2 0.6 copy.26
Async XLA Ops:
  92.0 1.4 %copy-start.2 = (f32[3,4,1024]{2,1,0:T(4,128)S(1)}, f32[3,4,1024]{2,1,0:T(4,128)}, u32[]{:S(2)}) copy-start(f32[3,4,1024]{2,1,0:T(4,128)} %get-tuple-element.41) | copy-start | bytes 147460
  93.5 0.7 copy-start.4
  93.5 1.2 %copy-start.1 = (f32[3,4,1024]{2,1,0:T(4,128)S(1)}, f32[3,4,1024]{2,1,0:T(4,128)}, u32[]{:S(2)}) copy-start(f32[3,4,1024]{2,1,0:T(4,128)} %get-tuple-element.43) | copy-start | bytes 147460
  94.7 0.8 copy-start
  95.5 0.7 copy-start.3
